TPU v7x, 256 devices: a whole 4x4x8 slice. The times are simulated.
256 devices in a mesh: det: 64 (over x, z, core), head: 4 (over y).
Axes of the slice: x: 4, y: 4, z: 8, core: 2. Of those that a mesh axis runs over, the one named last changes fastest.
Arguments:
- elements: bfloat16 [32768, 1024], P('det'), may hold values from -6 to 6
- element_types: int32 [32768], P('det'), may hold values from 0 to 1, as said below
- handover_counts: int32 [64, 64], replicated, may hold values from 0 to 16, as said below
- block_lists: int32 [256, 16], P('det'), may hold values from 0 to 255, as said below
- w_first: bfloat16 [2, 1024, 2048], P(None, None, 'head'), may hold values from -0.1875 to 0.1875
- w_second: bfloat16 [2, 2048, 1024], P(None, 'head'), may hold values from -0.125 to 0.125
- w_query: bfloat16 [1024, 1024], P(None, 'head'), may hold values from -3 to 3
- key_value_weight: bfloat16 [1024, 2, 256], P(None, None, 'head'), may hold values from -0.1875 to 0.1875
- attention_cotangent: bfloat16 [32768, 1024], P('det', 'head'), may hold values from -6 to 6
Outputs:
- attended: bfloat16 [32768, 1024], P('det', 'head')
- x_grad: bfloat16 [32768, 1024], P('det', 'head')
Inputs may be any that keep to these rules, and one draw needn't show every extreme that they name: `element_types`: of the 512 elements of each device of det, exactly 256 are of each type. `handover_counts`: row d, column e counts the elements that device d of det hands to device e; every row and every column sums to 512; some entries equal 16. `block_lists`: key block k is held by device k // 4 of det; the 16 entries of a query block may repeat; the lists of the 4 query blocks of one device together name exactly 1 block, counted with repeats, held by each device of det.
All inputs are finite; a program needn't handle non-finite values.
Results may differ from a plain program's by a relative error of at most 0.024.
The roundings to bfloat16 on the way count: a program that leaves them out, or rounds other values in their place, can miss the bound.
Values may be sent and summed in bfloat16 or wider, within the bound.
A program may use at most 64 MiB of HBM per device.

v0:
```python
import jax
import jax.numpy as jnp
from jax import lax
from jax.sharding import PartitionSpec as P

HEAD_SIZE = 64
BLOCK_ROWS = 128
LISTED_COUNT = 16
GROUP_HEADS = 4


def exclusive(counts, reduce_axis):
    return jnp.cumsum(counts, axis=reduce_axis, dtype=jnp.int32) - counts


def pack_rows(source_rows, starts, amounts, capacity):
    slot_ids = jnp.arange(capacity, dtype=jnp.int32)
    row_index = jnp.clip(starts[:, None] + slot_ids[None, :], 0, source_rows.shape[0] - 1)
    usable = slot_ids[None, :] < amounts[:, None]
    picked = source_rows[row_index.reshape(-1)].reshape(
        amounts.shape[0], capacity, source_rows.shape[1]
    )
    return jnp.where(usable[:, :, None], picked, jnp.zeros_like(picked))


def unpack_rows(received, starts, amounts, total_rows):
    peer_count, capacity = (received.shape[0], received.shape[1])
    within = jnp.arange(total_rows, dtype=jnp.int32)
    end_rows = starts + amounts
    peer_ids = jnp.sum(
        (end_rows[None, :] <= within[:, None]).astype(jnp.int32), axis=1, dtype=jnp.int32
    )
    slot_ids = within - starts[peer_ids]
    flattened = received.reshape(peer_count * capacity, received.shape[2])
    return flattened[peer_ids * capacity + slot_ids]


def attend(query_block_one, cotangent_block, key_block_rows, value_block_rows):
    score_scaling = HEAD_SIZE ** (-0.5)
    score_matrix = (
        jnp.einsum(
            "oenl,iel->enoi", query_block_one, key_block_rows, preferred_element_type=jnp.float32
        )
        * score_scaling
    )
    row_max = jnp.max(score_matrix, axis=-1, keepdims=True)
    exp_scores = jnp.exp(score_matrix - row_max)
    probability = exp_scores / jnp.sum(exp_scores, axis=-1, keepdims=True)
    probability_bfloat = probability.astype(jnp.bfloat16)
    attended = jnp.einsum(
        "vnys,svx->yvnx", probability_bfloat, value_block_rows, preferred_element_type=jnp.float32
    ).astype(jnp.bfloat16)
    probability_gradient = jnp.einsum(
        "oenl,iel->enoi", cotangent_block, value_block_rows, preferred_element_type=jnp.float32
    )
    row_delta = jnp.sum(probability * probability_gradient, axis=-1, keepdims=True)
    score_gradient = (probability * (probability_gradient - row_delta)).astype(jnp.bfloat16)
    query_gradient = (
        jnp.einsum(
            "vnys,svx->yvnx", score_gradient, key_block_rows, preferred_element_type=jnp.float32
        )
        * score_scaling
    ).astype(jnp.bfloat16)
    key_gradient = (
        jnp.einsum(
            "njtw,tnjs->wns", score_gradient, query_block_one, preferred_element_type=jnp.float32
        )
        * score_scaling
    )
    value_gradient = jnp.einsum(
        "njtw,tnjs->wns", probability_bfloat, cotangent_block, preferred_element_type=jnp.float32
    )
    return (attended, query_gradient, key_gradient, value_gradient)


def shards(
    elements,
    element_types,
    handover_counts,
    block_lists,
    w_first,
    w_second,
    w_query,
    key_value_weight,
    attention_cotangent,
):
    peer_count = lax.axis_size("det")
    my_index = lax.axis_index("det")
    row_count = elements.shape[0]
    model_width = elements.shape[1]
    capacity = 2 * row_count // peer_count
    starts = exclusive(handover_counts, 1)
    offsets = exclusive(handover_counts, 0)
    send_starts = lax.dynamic_index_in_dim(starts, my_index, 0, keepdims=False)
    send_counts = lax.dynamic_index_in_dim(handover_counts, my_index, 0, keepdims=False)
    recv_starts = lax.dynamic_index_in_dim(offsets, my_index, 1, keepdims=False)
    recv_counts = lax.dynamic_index_in_dim(handover_counts, my_index, 1, keepdims=False)
    type_count = w_first.shape[0]
    per_type = row_count // type_count
    type_order = jnp.argsort(element_types, stable=True)
    back_order = (
        jnp.zeros_like(type_order).at[type_order].set(jnp.arange(row_count, dtype=jnp.int32))
    )
    sorted_rows = elements[type_order].reshape(type_count, per_type, model_width)
    preact = jnp.einsum("trd,tdh->trh", sorted_rows, w_first, preferred_element_type=jnp.float32)
    hidden = jax.nn.gelu(preact).astype(jnp.bfloat16)
    sorted_mlp = jnp.einsum("trh,thd->trd", hidden, w_second, preferred_element_type=jnp.float32)
    partial_mlp = sorted_mlp.reshape(row_count, model_width)[back_order]
    mlp_sum = lax.psum(partial_mlp, "head")
    mixed = (elements.astype(jnp.float32) + mlp_sum).astype(jnp.bfloat16)
    outbound = pack_rows(mixed, send_starts, send_counts, capacity)
    inbound = lax.all_to_all(outbound, "det", split_axis=0, concat_axis=0, tiled=True)
    moved = unpack_rows(inbound, recv_starts, recv_counts, row_count)
    kv_width = key_value_weight.shape[2]
    key_value_flat = key_value_weight.reshape(model_width, 2 * kv_width)
    query_rows_all = jnp.dot(moved, w_query, preferred_element_type=jnp.float32).astype(
        jnp.bfloat16
    )
    key_value_pairs = jnp.dot(moved, key_value_flat, preferred_element_type=jnp.float32).astype(
        jnp.bfloat16
    )
    blocks_dev = row_count // BLOCK_ROWS
    slot_count = blocks_dev * LISTED_COUNT
    per_pair = slot_count // peer_count
    flat_list = block_lists.reshape(slot_count)
    owners = flat_list // blocks_dev
    local_ids = flat_list % blocks_dev
    slot_order = jnp.arange(slot_count, dtype=jnp.int32)
    earlier = (owners[:, None] == owners[None, :]) & (slot_order[None, :] < slot_order[:, None])
    slot_rank = jnp.sum(earlier.astype(jnp.int32), axis=1, dtype=jnp.int32)
    position = owners * per_pair + slot_rank
    requests = (
        jnp.zeros((slot_count,), jnp.int32)
        .at[position]
        .set(local_ids)
        .reshape(peer_count, per_pair)
    )
    wanted = lax.all_to_all(requests, "det", split_axis=0, concat_axis=0, tiled=True)
    all_keys = lax.all_gather(key_value_pairs, "det", axis=0, tiled=True)
    listed = all_keys.reshape(-1, BLOCK_ROWS, 2 * kv_width)[flat_list]
    listed = listed.reshape(blocks_dev, LISTED_COUNT * BLOCK_ROWS, 2 * kv_width)
    kv_heads = kv_width // HEAD_SIZE
    query_block_list = query_rows_all.reshape(
        blocks_dev, BLOCK_ROWS, kv_heads, GROUP_HEADS, HEAD_SIZE
    )
    cotangent_blocks = attention_cotangent.reshape(
        blocks_dev, BLOCK_ROWS, kv_heads, GROUP_HEADS, HEAD_SIZE
    )

    def one_block(inputs):
        query_block_one, cotangent_block, key_value_rows = inputs
        key_block_rows = key_value_rows[:, :kv_width].reshape(
            LISTED_COUNT * BLOCK_ROWS, kv_heads, HEAD_SIZE
        )
        value_block_rows = key_value_rows[:, kv_width:].reshape(
            LISTED_COUNT * BLOCK_ROWS, kv_heads, HEAD_SIZE
        )
        return attend(query_block_one, cotangent_block, key_block_rows, value_block_rows)

    attended, query_gradient, key_gradient, value_gradient = lax.map(
        one_block, (query_block_list, cotangent_blocks, listed)
    )
    slot_gradients = jnp.concatenate(
        [
            key_gradient.reshape(blocks_dev, LISTED_COUNT * BLOCK_ROWS, kv_width),
            value_gradient.reshape(blocks_dev, LISTED_COUNT * BLOCK_ROWS, kv_width),
        ],
        axis=2,
    )
    slot_gradients = slot_gradients.reshape(slot_count, BLOCK_ROWS, 2 * kv_width).astype(
        jnp.bfloat16
    )
    returned = (
        jnp.zeros_like(slot_gradients)
        .at[position]
        .set(slot_gradients)
        .reshape(peer_count, per_pair, BLOCK_ROWS, 2 * kv_width)
    )
    collected = lax.all_to_all(returned, "det", split_axis=0, concat_axis=0, tiled=True)
    collected = collected.reshape(slot_count, BLOCK_ROWS, 2 * kv_width).astype(jnp.float32)
    key_gradient_total = (
        jnp.zeros((blocks_dev, BLOCK_ROWS, 2 * kv_width), jnp.float32)
        .at[wanted.reshape(-1)]
        .add(collected)
    )
    key_bfloat = key_gradient_total.reshape(row_count, 2 * kv_width).astype(jnp.bfloat16)
    contract = (((1,), (1,)), ((), ()))
    partial_back = lax.dot_general(
        query_gradient.reshape(row_count, -1), w_query, contract, preferred_element_type=jnp.float32
    )
    partial_back = partial_back + lax.dot_general(
        key_bfloat, key_value_flat, contract, preferred_element_type=jnp.float32
    )
    back_sum = lax.psum(partial_back, "head").astype(jnp.bfloat16)
    outbound_back = pack_rows(back_sum, recv_starts, recv_counts, capacity)
    inbound_back = lax.all_to_all(outbound_back, "det", split_axis=0, concat_axis=0, tiled=True)
    upstream = unpack_rows(inbound_back, send_starts, send_counts, row_count)
    sorted_up = upstream[type_order].reshape(type_count, per_type, model_width)
    hidden_grad = jnp.einsum(
        "trd,thd->trh", sorted_up, w_second, preferred_element_type=jnp.float32
    )
    preact_grad = jax.vjp(jax.nn.gelu, preact)[1](hidden_grad)[0].astype(jnp.bfloat16)
    sorted_input = jnp.einsum(
        "trh,tdh->trd", preact_grad, w_first, preferred_element_type=jnp.float32
    )
    input_part = sorted_input.reshape(row_count, model_width)[back_order]
    input_share = lax.psum_scatter(input_part, "head", scatter_dimension=1, tiled=True)
    share_width = input_share.shape[1]
    own_upstream = lax.dynamic_slice_in_dim(
        upstream, lax.axis_index("head") * share_width, share_width, 1
    )
    x_grad = (own_upstream.astype(jnp.float32) + input_share).astype(jnp.bfloat16)
    return (attended.reshape(row_count, -1), x_grad)


def solution(mesh):
    return jax.shard_map(
        shards,
        mesh=mesh,
        in_specs=(
            P("det", None),
            P("det"),
            P(),
            P("det", None),
            P(None, None, "head"),
            P(None, "head", None),
            P(None, "head"),
            P(None, None, "head"),
            P("det", "head"),
        ),
        out_specs=(P("det", "head"), P("det", "head")),
        check_vma=False,
    )
```

profile of v0, /device:TPU:1, one launch (start us, length us, event | category | flops | bytes accessed | tf_op | source)
XLA Modules:
  0.0 602.9 jit_solution(14626544373594868727)
XLA Ops:
  7.2 4.6 sort.17
  11.8 2.4 scatter_custom_fusion
  14.3 4.1 gather_fusion
  18.4 2.3 fusion.99
  20.8 2.2 fusion.52
  22.9 5.3 gather_fusion.1
  29.4 66.3 %all-reduce.3.cloned.1.call-done = f32[512,1024]{1,0:T(8,128)} async-done(((f32[512,1024]{1,0:T(8,128)}), f32[512,1024]{1,0:T(8,128)}) %all-reduce.3.cloned.1.call-update) | async-done | bytes 2097168 | tf_op jit(solution)/shard_map/psum | solution.py:109
  95.8 2.2 add_convert_fusion
  98.0 5.4 gather_fusion.2
  103.4 3.2 broadcast_select_fusion.1
  106.6 11.0 %all-to-all-start = ((bf16[64,16,1024]{2,1,0:T(8,128)(2,1)}), bf16[64,16,1024]{2,1,0:T(8,128)(2,1)}, u32[]{:S(2)}, u32[]{:S(2)}) async-start(bf16[64,16,1024]{2,1,0:T(8,128)(2,1)} %broadcast_select_fusion.1), calls=%async_computation | async-start | bytes 4194304 | tf_op jit(solution)/shard_map/all_to_all | solution.py:112
  123.6 4.3 compare_select_fusion.12
  128.2 4.3 compare_select_fusion.6
  132.9 35.3 %select_select_fusion.1 = s32[512]{0:T(512)S(1)} fusion(pred[512]{0:T(512)(128)(4,1)S(1)} %get-tuple-element.224, pred[512]{0:T(512)(128)(4,1)S(1)} %get-tuple-element.223, pred[512]{0:T(512)(128)(4,1)S(1)} %get-tuple-element.222, pred[512]{0:T(512)(128)(4,1)S(1)} %get-tuple-element.221, pred[512]{0:T(512)(128)(4,1)S(1)} %get-tuple-element.220, ...), kind=kLoop, calls=%fused_computation.250 | loop fusion | flops 29184 | bytes 33508 | tf_op jit(solution)/shard_map/gather | solution.py:33
  168.3 35.6 %select_select_fusion = s32[512]{0:T(512)S(1)} fusion(pred[512]{0:T(512)(128)(4,1)S(1)} %get-tuple-element.167, pred[512]{0:T(512)(128)(4,1)S(1)} %get-tuple-element.166, pred[512]{0:T(512)(128)(4,1)S(1)} %get-tuple-element.165, pred[512]{0:T(512)(128)(4,1)S(1)} %get-tuple-element.164, pred[512]{0:T(512)(128)(4,1)S(1)} %get-tuple-element.163, ...), kind=kLoop, calls=%fused_computation.249 | loop fusion | flops 29184 | bytes 33508 | tf_op jit(solution)/shard_map/gather | solution.py:33
  204.0 4.6 gather_fusion.3
  210.1 10.0 %scatter_custom_fusion.1 = s32[64]{0:T(128)S(1)} fusion(s32[64]{0:T(128)S(1)} %get-tuple-element.385, s32[64]{0:T(128)S(1)} %get-tuple-element.383, s32[]{:T(128)} %constant.56.clone.1), kind=kCustom, calls=%fused_computation.271 | custom fusion | bytes 260 | tf_op jit(solution)/shard_map/scatter | solution.py:135
  220.8 10.3 %all-to-all-start.1 = ((s32[64,1,1]{2,1,0:T(1,128)}), s32[64,1,1]{2,1,0:T(1,128)S(1)}, u32[]{:S(2)}, u32[]{:S(2)}) async-start(s32[64,1,1]{2,1,0:T(1,128)} %copy.91), calls=%async_computation.1 | async-start | bytes 65536 | tf_op jit(solution)/shard_map/all_to_all | solution.py:138
  231.2 2.1 reshape.1340
  233.3 1.9 copy.88
  237.2 55.5 %all-gather.2.cloned.1.call-done = bf16[32768,128]{1,0:T(8,128)(2,1)} async-done(((bf16[512,128]{1,0:T(8,128)(2,1)}), bf16[32768,128]{1,0:T(8,128)(2,1)}) %all-gather.2.cloned.1.call-update) | async-done | bytes 8388624 | tf_op jit(solution)/shard_map/all_gather | solution.py:139
  292.7 5.6 gather_fusion.4
  298.3 41.0 %while.16 = (s32[]{:T(128)}, bf16[4,128,1,4,64]{1,4,3,2,0:T(8,128)(2,1)}, bf16[4,128,1,4,64]{1,4,3,2,0:T(8,128)(2,1)}, bf16[4,2048,1,64]{1,3,2,0:T(8,128)(2,1)},...) while((s32[]{:T(128)}, ...), condition=%wide.region_10.11_spmd, body=%wide.region_6.10_spmd.sunk | while | flops 830700032 | bytes 62289140 | solution.py:160
  307.0 1.6 fusion.136
  317.3 1.6 fusion.136
  339.4 2.0 copy.93
  342.9 2.0 copy.92
  346.5 3.1 pad_maximum_fusion
  349.5 4.2 copy.94
  353.7 1.9 broadcast_in_dim.43
  355.6 10.0 %scatter_fusion = bf16[64,128,128]{2,1,0:T(8,128)(2,1)} fusion(bf16[64,128,128]{2,1,0:T(8,128)(2,1)} %broadcast_in_dim.43, s32[64]{0:T(128)S(1)} %get-tuple-element.385, bf16[64,128,128]{2,1,0:T(8,128)(2,1)} %copy.94), kind=kCustom, calls=%fused_computation.11 | custom fusion | bytes 6291712 | tf_op jit(solution)/shard_map/scatter | solution.py:176
  365.6 6.0 %all-to-all-start.2 = ((bf16[64,1,128,128]{3,2,1,0:T(8,128)(2,1)}), bf16[64,1,128,128]{3,2,1,0:T(8,128)(2,1)}, u32[]{:S(2)}, u32[]{:S(2)}) async-start(bf16[64,1,128,128]{3,2,1,0:T(8,128)(2,1)} %bitcast.379), calls=%async_computation.2 | async-start | bytes 4194304 | tf_op jit(solution)/shard_map/all_to_all | solution.py:179
  373.3 49.4 %all-to-all-done.2 = bf16[64,1,128,128]{3,2,1,0:T(8,128)(2,1)} async-done(((bf16[64,1,128,128]{3,2,1,0:T(8,128)(2,1)}), bf16[64,1,128,128]{3,2,1,0:T(8,128)(2,1)}, u32[]{:S(2)}, u32[]{:S(2)}) %all-to-all-start.2) | async-done | bytes 2097184 | tf_op jit(solution)/shard_map/all_to_all | solution.py:179
  422.7 4.0 bitcast_convert_fusion
  426.8 8.8 %scatter_fusion.1 = f32[4,128,128]{2,1,0:T(8,128)S(1)} fusion(f32[4,128,128]{2,1,0:T(8,128)S(1)} %broadcast_in_dim.42, s32[64]{0:T(128)S(1)} %fusion.73, f32[64,128,128]{2,1,0:T(8,128)} %bitcast_convert_fusion), kind=kCustom, calls=%fused_computation.12 | custom fusion | flops 1048576 | bytes 12583168 | tf_op jit(solution)/shard_map/scatter-add | solution.py:184
  436.6 1.8 convolution_add_fusion
  438.5 42.7 %all-reduce.4 = bf16[512,1024]{1,0:T(8,128)(2,1)S(1)} all-reduce(f32[512,1024]{1,0:T(8,128)} %convolution_add_fusion), channel_id=1, replica_groups=mesh['det'=64,'head'=4] {'head'}, use_global_device_ids=true, to_apply=%region_15.16 | all-reduce | flops 524288 | bytes 3145728 | tf_op jit(solution)/shard_map/psum | solution.py:194
  481.2 5.4 gather_fusion.5
  486.6 3.2 broadcast_select_fusion
  489.8 8.1 %all-to-all-start.3 = ((bf16[64,16,1024]{2,1,0:T(8,128)(2,1)}), bf16[64,16,1024]{2,1,0:T(8,128)(2,1)}, u32[]{:S(2)}, u32[]{:S(2)}) async-start(bf16[64,16,1024]{2,1,0:T(8,128)(2,1)} %broadcast_select_fusion), calls=%async_computation.3 | async-start | bytes 4194304 | tf_op jit(solution)/shard_map/all_to_all | solution.py:196
  497.9 51.1 %all-to-all-done.3 = bf16[64,16,1024]{2,1,0:T(8,128)(2,1)} async-done(((bf16[64,16,1024]{2,1,0:T(8,128)(2,1)}), bf16[64,16,1024]{2,1,0:T(8,128)(2,1)}, u32[]{:S(2)}, u32[]{:S(2)}) %all-to-all-start.3) | async-done | bytes 2097184 | tf_op jit(solution)/shard_map/all_to_all | solution.py:196
  548.9 4.6 gather_fusion.6
  553.5 2.8 gather_fusion.7
  556.3 5.3 fusion.53
  561.7 5.2 gather_fusion.8
  568.9 2.2 reshape.1341
  571.1 23.1 %reduce-scatter.2.cloned.1.call-done = f32[512,256]{1,0:T(8,128)} async-done(((f32[512,1024]{1,0:T(8,128)}), f32[512,256]{1,0:T(8,128)}) %reduce-scatter.2.cloned.1.call-update) | async-done | bytes 524304 | tf_op jit(solution)/shard_map/reduce_scatter | solution.py:207
  594.2 1.8 add_convert_fusion.1
  (172 shorter events, 57.7 us)
Async XLA Ops:
  7.2 13.6 %copy-start = (bf16[2,512,1024]{2,1,0:T(8,128)(2,1)S(1)}, bf16[2,512,1024]{2,1,0:T(8,128)(2,1)}, u32[]{:S(2)}) copy-start(bf16[2,512,1024]{2,1,0:T(8,128)(2,1)} %param.16) | copy-start | bytes 6291460
  7.2 88.6 %all-reduce.3.cloned.1.call-start = ((), (), s32[]{:S(2)}) async-start(), calls=%async_computation.5 | async-start | bytes 4194304 | tf_op jit(solution)/shard_map/psum | solution.py:109
  11.8 6.6 %copy-start.13 = (s32[1024]{0:T(1024)}, s32[1024]{0:T(1024)S(1)}, u32[]{:S(2)}) copy-start(s32[1024]{0:T(1024)S(1)} %pad_clamp_fusion.4) | copy-start | bytes 12292
  14.3 8.6 %copy-start.15 = (s32[1024]{0:T(1024)}, s32[1024]{0:T(1024)S(1)}, u32[]{:S(2)}) copy-start(s32[1024]{0:T(1024)S(1)} %pad_clamp_fusion.3) | copy-start | bytes 12292
  20.7 2.2 copy-start.1
  28.2 0.8 copy-start.9
  106.6 97.4 %all-to-all-start = ((bf16[64,16,1024]{2,1,0:T(8,128)(2,1)}), bf16[64,16,1024]{2,1,0:T(8,128)(2,1)}, u32[]{:S(2)}, u32[]{:S(2)}) async-start(bf16[64,16,1024]{2,1,0:T(8,128)(2,1)} %broadcast_select_fusion.1), calls=%async_computation | async-start | bytes 4194304 | tf_op jit(solution)/shard_map/all_to_all | solution.py:112
  117.6 175.2 %all-gather.2.cloned.1.call-start = ((), (), s32[]{:S(2)}) async-start(), calls=%async_computation.6 | async-start | bytes 8519680 | tf_op jit(solution)/shard_map/all_gather | solution.py:139
  203.9 4.7 copy-start.6
  204.0 5.8 copy-start.17
  220.8 144.7 %all-to-all-start.1 = ((s32[64,1,1]{2,1,0:T(1,128)}), s32[64,1,1]{2,1,0:T(1,128)S(1)}, u32[]{:S(2)}, u32[]{:S(2)}) async-start(s32[64,1,1]{2,1,0:T(1,128)} %copy.91), calls=%async_computation.1 | async-start | bytes 65536 | tf_op jit(solution)/shard_map/all_to_all | solution.py:138
  300.4 1.2 copy-start.4
  300.4 1.3 copy-start.10
  302.6 1.3 copy-start.5
  303.9 1.2 copy-start.2
  305.9 1.1 copy-start.3
  310.6 1.2 copy-start.4
  310.7 1.3 copy-start.10
  312.9 1.3 copy-start.5
  314.2 1.2 copy-start.2
  316.2 1.1 copy-start.3
  320.9 1.2 copy-start.4
  320.9 1.3 copy-start.10
  323.1 1.3 copy-start.5
  324.4 1.2 copy-start.2
  326.4 1.1 copy-start.3
  331.2 1.2 copy-start.4
  331.2 1.3 copy-start.10
  333.4 1.3 copy-start.5
  334.7 1.2 copy-start.2
  336.7 1.1 copy-start.3
  365.6 7.6 %copy-start.12 = (bf16[4,128,1,4,64]{1,4,3,2,0:T(8,128)(2,1)S(1)}, bf16[4,128,1,4,64]{1,4,3,2,0:T(8,128)(2,1)}, u32[]{:S(2)}) copy-start(bf16[4,128,1,4,64]{1,4,3,2,0:T(8,128)(2,1)} %get-tuple-element.50) | copy-start | bytes 786436
  365.6 57.2 %all-to-all-start.2 = ((bf16[64,1,128,128]{3,2,1,0:T(8,128)(2,1)}), bf16[64,1,128,128]{3,2,1,0:T(8,128)(2,1)}, u32[]{:S(2)}, u32[]{:S(2)}) async-start(bf16[64,1,128,128]{3,2,1,0:T(8,128)(2,1)} %bitcast.379), calls=%async_computation.2 | async-start | bytes 4194304 | tf_op jit(solution)/shard_map/all_to_all | solution.py:179
  426.8 8.8 %copy-start.7 = (bf16[1024,2,64]{0,2,1:T(8,128)(2,1)S(1)}, bf16[1024,2,64]{0,2,1:T(8,128)(2,1)}, u32[]{:S(2)}) copy-start(bf16[1024,2,64]{0,2,1:T(8,128)(2,1)} %param.18) | copy-start | bytes 786436
  435.6 1.0 copy-start.8
  489.8 59.2 %all-to-all-start.3 = ((bf16[64,16,1024]{2,1,0:T(8,128)(2,1)}), bf16[64,16,1024]{2,1,0:T(8,128)(2,1)}, u32[]{:S(2)}, u32[]{:S(2)}) async-start(bf16[64,16,1024]{2,1,0:T(8,128)(2,1)} %broadcast_select_fusion), calls=%async_computation.3 | async-start | bytes 4194304 | tf_op jit(solution)/shard_map/all_to_all | solution.py:196
  497.8 96.4 %reduce-scatter.2.cloned.1.call-start = ((), (), s32[]{:S(2)}) async-start(), calls=%async_computation.7 | async-start | bytes 2621440 | tf_op jit(solution)/shard_map/reduce_scatter | solution.py:207
  548.9 4.6 copy-start.14
  556.3 5.3 copy-start.16
  566.9 0.9 copy-start.11
Sparse Core Ops, SparseCore 0:
  28.3 67.4 all-reduce.2
  209.9 82.8 all-gather.1
  567.0 27.1 reduce-scatter.1
where the time goes:
time: 614 us; the launch traced here: 603 us
  waiting for transfers between devices  245 us (40%)
  other arithmetic  121 us (20%)
  local copies, waits for them, and re-layouts  103 us (17%)
  blocking collectives  42.7 us (7%)
  matrix products  40.3 us (7%)
  starting transfers between devices  35.6 us (6%)
  between operations  14.6 us (2%)
    gather x6, other arithmetic, unpack_rows(): slot_ids = within - starts[peer_ids]  80.3 us
    psum x1, waiting for transfers between devices, shards(): mlp_sum = lax.psum(partial_mlp, 'head')  66.3 us
    all_gather x1, waiting for transfers between devices, shards(): all_keys = lax.all_gather(key_value_pairs, 'det', axis=0, tiled=True)  55.5 us
    all_to_all x1, waiting for transfers between devices, shards(): lax.all_to_all(outbound_back, 'det', split_axis=0, concat_axis=0, tiled=T...  51.1 us
    all_to_all x1, waiting for transfers between devices, shards(): lax.all_to_all(returned, 'det', split_axis=0, concat_axis=0, tiled=True)  49.4 us
    psum x1, blocking collectives, shards(): back_sum = lax.psum(partial_back, 'head').astype(jnp.bfloat16)  42.7 us
    reduce_scatter x1, waiting for transfers between devices, shards(): lax.psum_scatter(input_part, 'head', scatter_dimension=1, tiled=True)  23.1 us
  transfers between devices with their start and end apart: 7, of which 5 were waited for; matrix products, arithmetic and copies ran while one was open for 30% of the time, Pallas kernels for 0%

commit v1 on v0

--- a/solution.py
+++ b/solution.py
@@ -106,7 +106,9 @@
     hidden = jax.nn.gelu(preact).astype(jnp.bfloat16)
     sorted_mlp = jnp.einsum("trh,thd->trd", hidden, w_second, preferred_element_type=jnp.float32)
     partial_mlp = sorted_mlp.reshape(row_count, model_width)[back_order]
-    mlp_sum = lax.psum(partial_mlp, "head")
+    mlp_sum = partial_mlp
+    for hop in (1, 2):
+        mlp_sum = mlp_sum + lax.ppermute(mlp_sum, "head", [(dev, dev ^ hop) for dev in range(4)])
     mixed = (elements.astype(jnp.float32) + mlp_sum).astype(jnp.bfloat16)
     outbound = pack_rows(mixed, send_starts, send_counts, capacity)
     inbound = lax.all_to_all(outbound, "det", split_axis=0, concat_axis=0, tiled=True)

time: 614 us -> 661 us (1.077)
  waiting for transfers between devices: 245 us -> 279 us
  starting transfers between devices: 35.6 us -> 56.6 us
  local copies, waits for them, and re-layouts: 103 us -> 93.1 us
    ppermute x0 -> x2, waiting for transfers between devices: none -> 88.6 us  [shards(): lax.ppermute(mlp_sum, 'head', [(dev, dev ^ hop) for dev in range(4)])]
    psum x1 -> x0, waiting for transfers between devices: 66.3 us -> none  [shards(): mlp_sum = lax.psum(partial_mlp, 'head')]
    all_gather x1, starting transfers between devices: 0.04 us -> 12.2 us  [shards(): all_keys = lax.all_gather(key_value_pairs, 'det', axis=0, tiled=True)]
    all_gather x1, waiting for transfers between devices: 55.5 us -> 66.4 us  [shards(): all_keys = lax.all_gather(key_value_pairs, 'det', axis=0, tiled=True)]
    scatter x1, local copies, waits for them, and re-layouts: 10 us -> 0.77 us  [shards(): requests = jnp.zeros((slot_count,), jnp.int32).at[position].set(local_ids...]
  transfers between devices with their start and end apart: 7 -> 8, of which waited for: 5 -> 6; matrix products, arithmetic and copies ran while one was open for 30% -> 26% of each run, Pallas kernels for 0% -> 0%
where the time goes in v1:
time: 661 us; the launch traced here: 652 us
  waiting for transfers between devices  279 us (42%)
  other arithmetic  125 us (19%)
  local copies, waits for them, and re-layouts  93.1 us (14%)
  starting transfers between devices  56.6 us (9%)
  blocking collectives  42.7 us (6%)
  matrix products  40.4 us (6%)
  between operations  14.9 us (2%)
    ppermute x2, waiting for transfers between devices, shards(): lax.ppermute(mlp_sum, 'head', [(dev, dev ^ hop) for dev in range(4)])  88.6 us
    gather x6, other arithmetic, unpack_rows(): slot_ids = within - starts[peer_ids]  80.3 us
    all_gather x1, waiting for transfers between devices, shards(): all_keys = lax.all_gather(key_value_pairs, 'det', axis=0, tiled=True)  66.4 us
    all_to_all x1, waiting for transfers between devices, shards(): lax.all_to_all(outbound_back, 'det', split_axis=0, concat_axis=0, tiled=T...  51.1 us
    all_to_all x1, waiting for transfers between devices, shards(): lax.all_to_all(returned, 'det', split_axis=0, concat_axis=0, tiled=True)  49.4 us
    psum x1, blocking collectives, shards(): back_sum = lax.psum(partial_back, 'head').astype(jnp.bfloat16)  42.7 us
    reduce_scatter x1, waiting for transfers between devices, shards(): lax.psum_scatter(input_part, 'head', scatter_dimension=1, tiled=True)  23.1 us
    all_to_all x1, starting transfers between devices, shards(): lax.all_to_all(outbound, 'det', split_axis=0, concat_axis=0, tiled=True)  14 us
  transfers between devices with their start and end apart: 8, of which 6 were waited for; matrix products, arithmetic and copies ran while one was open for 26% of the time, Pallas kernels for 0%

profile of v1, /device:TPU:1, one launch (start us, length us, event | category | flops | bytes accessed | tf_op | source)
XLA Modules:
  0.0 651.6 jit_solution(3572705913856642082)
XLA Ops:
  7.2 4.6 sort.17
  11.8 2.4 scatter_custom_fusion
  14.3 4.1 gather_fusion
  18.4 2.3 fusion.99
  20.7 2.2 fusion.52
  22.9 5.2 gather_fusion.1
  28.1 2.1 collective-permute-start
  30.3 44.5 %collective-permute-done = f32[512,1024]{1,0:T(8,128)S(1)} collective-permute-done((f32[512,1024]{1,0:T(8,128)}, f32[512,1024]{1,0:T(8,128)S(1)}, u32[]{:S(2)}, u32[]{:S(2)}) %collective-permute-start) | collective-permute-done | bytes 2097184 | tf_op jit(solution)/shard_map/ppermute | solution.py:111
  74.8 3.3 add.257
  78.0 3.9 collective-permute-start.1
  82.4 44.1 %collective-permute-done.1 = f32[512,1024]{1,0:T(8,128)} collective-permute-done((f32[512,1024]{1,0:T(8,128)}, f32[512,1024]{1,0:T(8,128)}, u32[]{:S(2)}, u32[]{:S(2)}) %collective-permute-start.1) | collective-permute-done | bytes 2097184 | tf_op jit(solution)/shard_map/ppermute | solution.py:111
  126.5 3.1 add_convert_fusion
  129.6 5.4 gather_fusion.2
  135.0 3.2 broadcast_select_fusion.1
  138.2 14.0 %all-to-all-start = ((bf16[64,16,1024]{2,1,0:T(8,128)(2,1)}), bf16[64,16,1024]{2,1,0:T(8,128)(2,1)}, u32[]{:S(2)}, u32[]{:S(2)}) async-start(bf16[64,16,1024]{2,1,0:T(8,128)(2,1)} %broadcast_select_fusion.1), calls=%async_computation | async-start | bytes 4194304 | tf_op jit(solution)/shard_map/all_to_all | solution.py:114
  152.2 12.2 %all-gather.2.cloned.1.call-start = ((), (), s32[]{:S(2)}) async-start(), calls=%async_computation.5 | async-start | bytes 8519680 | tf_op jit(solution)/shard_map/all_gather | solution.py:141
  170.3 4.3 compare_select_fusion.12
  174.9 4.3 compare_select_fusion.6
  179.7 35.3 %select_select_fusion.1 = s32[512]{0:T(512)S(1)} fusion(pred[512]{0:T(512)(128)(4,1)S(1)} %get-tuple-element.224, pred[512]{0:T(512)(128)(4,1)S(1)} %get-tuple-element.223, pred[512]{0:T(512)(128)(4,1)S(1)} %get-tuple-element.222, pred[512]{0:T(512)(128)(4,1)S(1)} %get-tuple-element.221, pred[512]{0:T(512)(128)(4,1)S(1)} %get-tuple-element.220, ...), kind=kLoop, calls=%fused_computation.250 | loop fusion | flops 29184 | bytes 33508 | tf_op jit(solution)/shard_map/gather | solution.py:33
  215.0 35.6 %select_select_fusion = s32[512]{0:T(512)S(1)} fusion(pred[512]{0:T(512)(128)(4,1)S(1)} %get-tuple-element.167, pred[512]{0:T(512)(128)(4,1)S(1)} %get-tuple-element.166, pred[512]{0:T(512)(128)(4,1)S(1)} %get-tuple-element.165, pred[512]{0:T(512)(128)(4,1)S(1)} %get-tuple-element.164, pred[512]{0:T(512)(128)(4,1)S(1)} %get-tuple-element.163, ...), kind=kLoop, calls=%fused_computation.249 | loop fusion | flops 29184 | bytes 33508 | tf_op jit(solution)/shard_map/gather | solution.py:33
  250.7 4.6 gather_fusion.3
  258.3 10.3 %all-to-all-start.1 = ((s32[64,1,1]{2,1,0:T(1,128)}), s32[64,1,1]{2,1,0:T(1,128)S(1)}, u32[]{:S(2)}, u32[]{:S(2)}) async-start(s32[64,1,1]{2,1,0:T(1,128)} %copy.91), calls=%async_computation.1 | async-start | bytes 65536 | tf_op jit(solution)/shard_map/all_to_all | solution.py:140
  268.7 2.1 reshape.1340
  270.8 1.9 copy.88
  274.7 66.4 %all-gather.2.cloned.1.call-done = bf16[32768,128]{1,0:T(8,128)(2,1)} async-done(((bf16[512,128]{1,0:T(8,128)(2,1)}), bf16[32768,128]{1,0:T(8,128)(2,1)}) %all-gather.2.cloned.1.call-update) | async-done | bytes 8388624 | tf_op jit(solution)/shard_map/all_gather | solution.py:141
  341.1 5.6 gather_fusion.4
  346.7 41.0 %while.16 = (s32[]{:T(128)}, bf16[4,128,1,4,64]{1,4,3,2,0:T(8,128)(2,1)}, bf16[4,128,1,4,64]{1,4,3,2,0:T(8,128)(2,1)}, bf16[4,2048,1,64]{1,3,2,0:T(8,128)(2,1)},...) while((s32[]{:T(128)}, ...), condition=%wide.region_9.10_spmd, body=%wide.region_5.9_spmd.sunk | while | flops 830700032 | bytes 62289140 | solution.py:162
  387.7 2.0 copy.93
  391.3 2.0 copy.92
  394.8 3.1 pad_maximum_fusion
  397.9 4.2 copy.94
  402.1 1.9 broadcast_in_dim.43
  404.0 10.0 %scatter_fusion = bf16[64,128,128]{2,1,0:T(8,128)(2,1)} fusion(bf16[64,128,128]{2,1,0:T(8,128)(2,1)} %broadcast_in_dim.43, s32[64]{0:T(128)S(1)} %get-tuple-element.385, bf16[64,128,128]{2,1,0:T(8,128)(2,1)} %copy.94), kind=kCustom, calls=%fused_computation.11 | custom fusion | bytes 6291712 | tf_op jit(solution)/shard_map/scatter | solution.py:178
  413.9 6.1 all-to-all-start.2
  421.7 49.4 %all-to-all-done.2 = bf16[64,1,128,128]{3,2,1,0:T(8,128)(2,1)} async-done(((bf16[64,1,128,128]{3,2,1,0:T(8,128)(2,1)}), bf16[64,1,128,128]{3,2,1,0:T(8,128)(2,1)}, u32[]{:S(2)}, u32[]{:S(2)}) %all-to-all-start.2) | async-done | bytes 2097184 | tf_op jit(solution)/shard_map/all_to_all | solution.py:181
  471.1 4.0 bitcast_convert_fusion
  475.2 8.8 %scatter_fusion.1 = f32[4,128,128]{2,1,0:T(8,128)S(1)} fusion(f32[4,128,128]{2,1,0:T(8,128)S(1)} %broadcast_in_dim.42, s32[64]{0:T(128)S(1)} %fusion.73, f32[64,128,128]{2,1,0:T(8,128)} %bitcast_convert_fusion), kind=kCustom, calls=%fused_computation.12 | custom fusion | flops 1048576 | bytes 12583168 | tf_op jit(solution)/shard_map/scatter-add | solution.py:186
  486.9 42.7 %all-reduce.1 = bf16[512,1024]{1,0:T(8,128)(2,1)S(1)} all-reduce(f32[512,1024]{1,0:T(8,128)} %convolution_add_fusion), channel_id=1, replica_groups=mesh['det'=64,'head'=4] {'head'}, use_global_device_ids=true, to_apply=%region_14.15 | all-reduce | flops 524288 | bytes 3145728 | tf_op jit(solution)/shard_map/psum | solution.py:196
  529.6 5.4 gather_fusion.5
  535.0 3.2 broadcast_select_fusion
  538.1 8.1 %all-to-all-start.3 = ((bf16[64,16,1024]{2,1,0:T(8,128)(2,1)}), bf16[64,16,1024]{2,1,0:T(8,128)(2,1)}, u32[]{:S(2)}, u32[]{:S(2)}) async-start(bf16[64,16,1024]{2,1,0:T(8,128)(2,1)} %broadcast_select_fusion), calls=%async_computation.3 | async-start | bytes 4194304 | tf_op jit(solution)/shard_map/all_to_all | solution.py:198
  546.3 51.1 %all-to-all-done.3 = bf16[64,16,1024]{2,1,0:T(8,128)(2,1)} async-done(((bf16[64,16,1024]{2,1,0:T(8,128)(2,1)}), bf16[64,16,1024]{2,1,0:T(8,128)(2,1)}, u32[]{:S(2)}, u32[]{:S(2)}) %all-to-all-start.3) | async-done | bytes 2097184 | tf_op jit(solution)/shard_map/all_to_all | solution.py:198
  597.3 4.6 gather_fusion.6
  601.9 2.8 gather_fusion.7
  604.7 5.3 fusion.53
  610.0 5.2 gather_fusion.8
  617.3 2.2 reshape.1341
  619.4 23.1 %reduce-scatter.2.cloned.1.call-done = f32[512,256]{1,0:T(8,128)} async-done(((f32[512,1024]{1,0:T(8,128)}), f32[512,256]{1,0:T(8,128)}) %reduce-scatter.2.cloned.1.call-update) | async-done | bytes 524304 | tf_op jit(solution)/shard_map/reduce_scatter | solution.py:209
  (174 shorter events, 64.4 us)
Async XLA Ops:
  7.2 13.5 %copy-start = (bf16[2,512,1024]{2,1,0:T(8,128)(2,1)S(1)}, bf16[2,512,1024]{2,1,0:T(8,128)(2,1)}, u32[]{:S(2)}) copy-start(bf16[2,512,1024]{2,1,0:T(8,128)(2,1)} %param.16) | copy-start | bytes 6291460
  11.8 6.6 %copy-start.13 = (s32[1024]{0:T(1024)}, s32[1024]{0:T(1024)S(1)}, u32[]{:S(2)}) copy-start(s32[1024]{0:T(1024)S(1)} %pad_clamp_fusion.4) | copy-start | bytes 12292
  14.3 8.7 %copy-start.15 = (s32[1024]{0:T(1024)}, s32[1024]{0:T(1024)S(1)}, u32[]{:S(2)}) copy-start(s32[1024]{0:T(1024)S(1)} %pad_clamp_fusion.3) | copy-start | bytes 12292
  20.7 2.2 copy-start.1
  28.1 53.7 %copy-start.9 = (s32[64,64]{1,0:T(8,128)S(1)}, s32[64,64]{1,0:T(8,128)}, u32[]{:S(2)}) copy-start(s32[64,64]{1,0:T(8,128)} %param.13) | copy-start | bytes 49156
  28.1 46.6 %collective-permute-start = (f32[512,1024]{1,0:T(8,128)}, f32[512,1024]{1,0:T(8,128)S(1)}, u32[]{:S(2)}, u32[]{:S(2)}) collective-permute-start(f32[512,1024]{1,0:T(8,128)} %gather_fusion.1), channel_id=1, source_target_pairs={{0,1},{1,0},{2,3},{3,2},{4,5},{5,4},{6,7},{7,6},{8,9},{9,8},{10,11... | collective-permute-start | bytes 6291464 | tf_op jit(solution)/shard_map/ppermute | solution.py:111
  78.0 48.5 %collective-permute-start.1 = (f32[512,1024]{1,0:T(8,128)}, f32[512,1024]{1,0:T(8,128)}, u32[]{:S(2)}, u32[]{:S(2)}) collective-permute-start(f32[512,1024]{1,0:T(8,128)} %add.257), channel_id=1, source_target_pairs={{0,2},{1,3},{2,0},{3,1},{4,6},{5,7},{6,4},{7,5},{8,10},{9,11},{10,... | collective-permute-start | bytes 6291464 | tf_op jit(solution)/shard_map/ppermute | solution.py:111
  138.2 112.5 %all-to-all-start = ((bf16[64,16,1024]{2,1,0:T(8,128)(2,1)}), bf16[64,16,1024]{2,1,0:T(8,128)(2,1)}, u32[]{:S(2)}, u32[]{:S(2)}) async-start(bf16[64,16,1024]{2,1,0:T(8,128)(2,1)} %broadcast_select_fusion.1), calls=%async_computation | async-start | bytes 4194304 | tf_op jit(solution)/shard_map/all_to_all | solution.py:114
  152.2 189.0 %all-gather.2.cloned.1.call-start = ((), (), s32[]{:S(2)}) async-start(), calls=%async_computation.5 | async-start | bytes 8519680 | tf_op jit(solution)/shard_map/all_gather | solution.py:141
  250.7 4.7 copy-start.6
  250.7 5.8 copy-start.17
  258.3 155.6 %all-to-all-start.1 = ((s32[64,1,1]{2,1,0:T(1,128)}), s32[64,1,1]{2,1,0:T(1,128)S(1)}, u32[]{:S(2)}, u32[]{:S(2)}) async-start(s32[64,1,1]{2,1,0:T(1,128)} %copy.91), calls=%async_computation.1 | async-start | bytes 65536 | tf_op jit(solution)/shard_map/all_to_all | solution.py:140
  348.8 1.2 copy-start.4
  348.8 1.3 copy-start.10
  351.0 1.3 copy-start.5
  352.3 1.2 copy-start.2
  354.3 1.1 copy-start.3
  359.0 1.2 copy-start.4
  359.0 1.3 copy-start.10
  361.3 1.3 copy-start.5
  362.6 1.2 copy-start.2
  364.5 1.1 copy-start.3
  369.3 1.2 copy-start.4
  369.3 1.3 copy-start.10
  371.5 1.3 copy-start.5
  372.8 1.2 copy-start.2
  374.8 1.1 copy-start.3
  379.5 1.2 copy-start.4
  379.5 1.3 copy-start.10
  381.8 1.3 copy-start.5
  383.1 1.2 copy-start.2
  385.1 1.1 copy-start.3
  413.9 7.6 %copy-start.12 = (bf16[4,128,1,4,64]{1,4,3,2,0:T(8,128)(2,1)S(1)}, bf16[4,128,1,4,64]{1,4,3,2,0:T(8,128)(2,1)}, u32[]{:S(2)}) copy-start(bf16[4,128,1,4,64]{1,4,3,2,0:T(8,128)(2,1)} %get-tuple-element.50) | copy-start | bytes 786436
  413.9 57.2 %all-to-all-start.2 = ((bf16[64,1,128,128]{3,2,1,0:T(8,128)(2,1)}), bf16[64,1,128,128]{3,2,1,0:T(8,128)(2,1)}, u32[]{:S(2)}, u32[]{:S(2)}) async-start(bf16[64,1,128,128]{3,2,1,0:T(8,128)(2,1)} %bitcast.379), calls=%async_computation.2 | async-start | bytes 4194304 | tf_op jit(solution)/shard_map/all_to_all | solution.py:181
  475.2 8.8 %copy-start.7 = (bf16[1024,2,64]{0,2,1:T(8,128)(2,1)S(1)}, bf16[1024,2,64]{0,2,1:T(8,128)(2,1)}, u32[]{:S(2)}) copy-start(bf16[1024,2,64]{0,2,1:T(8,128)(2,1)} %param.18) | copy-start | bytes 786436
  484.0 1.0 copy-start.8
  538.1 59.2 %all-to-all-start.3 = ((bf16[64,16,1024]{2,1,0:T(8,128)(2,1)}), bf16[64,16,1024]{2,1,0:T(8,128)(2,1)}, u32[]{:S(2)}, u32[]{:S(2)}) async-start(bf16[64,16,1024]{2,1,0:T(8,128)(2,1)} %broadcast_select_fusion), calls=%async_computation.3 | async-start | bytes 4194304 | tf_op jit(solution)/shard_map/all_to_all | solution.py:198
  546.2 96.4 %reduce-scatter.2.cloned.1.call-start = ((), (), s32[]{:S(2)}) async-start(), calls=%async_computation.6 | async-start | bytes 2621440 | tf_op jit(solution)/shard_map/reduce_scatter | solution.py:209
  597.3 4.6 copy-start.14
  604.7 5.3 copy-start.16
  615.2 0.9 copy-start.11
Sparse Core Ops, SparseCore 0:
  256.6 84.4 all-gather.1
  615.4 27.1 reduce-scatter.1
